TPU v7x, 32 devices: a whole 2x2x4 slice. The times are simulated.
32 devices in a mesh: groups: 2 (over y), seq: 4 (over z), strand: 2 (over core), chan: 2 (over x).
Axes of the slice: x: 2, y: 2, z: 4, core: 2. Of those that a mesh axis runs over, the one named last changes fastest.
Arguments:
- seq_in: bfloat16 [2, 6144, 512], P('strand', ('groups', 'seq', 'chan')), parts along dimension 1, may hold values from -6 to 6
- conv_norm: float32 [2, 512], replicated, may hold values from 0.1 to 1.9
- conv_weight: bfloat16 [2, 3, 512, 512], P(None, None, None, ('seq', 'chan')), may hold values from -0.15625 to 0.15625
- ff_norm: float32 [2, 512], replicated, may hold values from 0.1 to 1.9
- up_weight: bfloat16 [2, 512, 2048], P(None, None, ('seq', 'chan')), may hold values from -0.25 to 0.25
- down_weight: bfloat16 [2, 2048, 512], P(None, ('seq', 'chan')), may hold values from -0.125 to 0.125
- head_norm: float32 [512], replicated, may hold values from 0.1 to 1.9
- value_weight: bfloat16 [512, 512], replicated, may hold values from -0.25 to 0.25
- gate_weight: bfloat16 [512, 512], replicated, may hold values from -0.25 to 0.25
- out_weight: bfloat16 [512, 512], replicated, may hold values from -0.25 to 0.25
Outputs:
- strand_out: bfloat16 [2, 6144, 512], P('strand', ('groups', 'seq', 'chan')), parts along dimension 1
There are 2 independent parts, one for each index of `groups`. A program takes and returns all parts, laid end to end along the dimension named above; an argument that names none is the same for every part. Nothing has to cross between parts.
All inputs are finite; a program needn't handle non-finite values.
Results may differ from a plain program's by a relative error of at most 0.015.
Values may be sent and summed in bfloat16 or wider, within the bound.
No kernel may reach another device: no remote copies, remote signals or barrier semaphores. Data moves between devices by JAX's collectives and lax.ppermute only.
A program may use at most 64 MiB of HBM per device.

v0:
```python
import jax
import jax.numpy as jnp
from jax import lax
from jax.sharding import PartitionSpec as P


def passed_along(value, axis, steps):
    count = lax.axis_size(axis)
    initial, last = (max(0, -steps), min(count, count - steps))
    return lax.ppermute(value, axis, [(source, source + steps) for source in range(initial, last)])


def swapped(x, axis, stride):
    return lax.ppermute(x, axis, [(i, i ^ 1 << stride) for i in range(lax.axis_size(axis))])


def normalize(values, gain):
    return values * lax.rsqrt(jnp.mean(values * values, axis=-1, keepdims=True) + 1e-06) * gain


def matmul(left, right):
    return jnp.dot(left, right, preferred_element_type=jnp.float32)


def local(
    seq_in,
    conv_norm,
    conv_weight,
    ff_norm,
    up_weight,
    down_weight,
    head_norm,
    value_weight,
    gate_weight,
    out_weight,
):
    state = seq_in[0].astype(jnp.float32)
    seq_count = lax.axis_size("seq")
    for block in range(conv_weight.shape[0]):
        reach = min(2**block, seq_count // 2)
        normed = normalize(state, conv_norm[block]).astype(jnp.bfloat16)
        before = passed_along(normed, "seq", reach)
        after = passed_along(normed, "seq", -reach)
        piece = lax.all_gather(conv_weight[block], ("seq", "chan"), axis=2, tiled=True)
        total = matmul(before, piece[0]) + matmul(normed, piece[1]) + matmul(after, piece[2])
        conv = total.astype(jnp.bfloat16)
        state = state + conv.astype(jnp.float32)
        mixed = normalize(state, ff_norm[block]).astype(jnp.bfloat16)
        hidden = jax.nn.gelu(
            matmul(mixed, lax.all_gather(up_weight[block], ("seq", "chan"), axis=1, tiled=True))
        ).astype(jnp.bfloat16)
        state = state + matmul(
            hidden, lax.all_gather(down_weight[block], ("seq", "chan"), axis=0, tiled=True)
        )
    final = normalize(state, head_norm).astype(jnp.bfloat16)
    value = matmul(final, value_weight)
    bit_count = (seq_count * lax.axis_size("chan")).bit_length() - 1
    opposite = swapped(final, "strand", 0)
    for digit in range(bit_count):
        opposite = swapped(opposite, ("seq", "chan"), digit)
    opposite = jnp.flip(opposite, 0)
    mirrored = matmul(opposite, gate_weight).astype(jnp.bfloat16)
    gated = (value * jax.nn.sigmoid(mirrored.astype(jnp.float32))).astype(jnp.bfloat16)
    result = matmul(gated, out_weight)
    return result.astype(jnp.bfloat16)[None]


def solution(mesh):
    in_specs = (
        P("strand", ("groups", "seq", "chan"), None),
        P(),
        P(None, None, None, ("seq", "chan")),
        P(),
        P(None, None, ("seq", "chan")),
        P(None, ("seq", "chan"), None),
        P(),
        P(),
        P(),
        P(),
    )
    out_specs = P("strand", ("groups", "seq", "chan"), None)
    return jax.shard_map(local, mesh=mesh, in_specs=in_specs, out_specs=out_specs, check_vma=False)
```

profile of v0, /device:TPU:0, one launch (start us, length us, event | category | flops | bytes accessed | tf_op | source)
XLA Modules:
  0.0 376.3 jit_solution(10085259237027235437)
XLA Ops:
  6.5 0.0 copy-start
  6.5 0.0 all-gather.13.cloned.1.call-start
  6.6 1.9 fusion.86
  8.5 0.0 all-gather.13.cloned.1.call-update
  8.5 0.0 copy-start.6
  8.5 0.0 all-gather.15.cloned.1.call-start
  8.6 1.9 fusion.84
  10.5 0.0 all-gather.15.cloned.1.call-update
  10.5 0.0 all-gather.17.cloned.1.call-start
  10.5 0.0 copy-done.4
  10.5 0.8 fusion.85
  11.4 0.0 all-gather.17.cloned.1.call-update
  11.4 0.0 all-gather.19.cloned.1.call-start
  11.4 0.5 all-gather.19.cloned.1.call-update
  12.0 0.0 all-gather.21.cloned.1.call-start
  12.0 0.5 all-gather.21.cloned.1.call-update
  12.6 0.0 all-gather.23.cloned.1.call-start
  12.6 0.0 copy-done.1
  12.6 0.2 fusion.55
  12.8 0.0 copy-done.5
  12.8 0.2 fusion.57
  13.0 1.3 collective-permute-start.1
  14.3 0.0 all-gather.23.cloned.1.call-update
  14.3 5.6 %collective-permute-start = (bf16[384,512]{1,0:T(8,128)(2,1)S(1)}, bf16[384,512]{1,0:T(8,128)(2,1)S(1)}, u32[]{:S(2)}, u32[]{:S(2)}) collective-permute-start(bf16[384,512]{1,0:T(8,128)(2,1)S(1)} %fusion.57), channel_id=1, source_target_pairs={{0,4},{4,8},{8,12},{1,5},{5,9},{9,13},{2,6},{6,10},{10,14},{3,7},{... | collective-permute-start | bytes 1179656 | tf_op jit(solution)/shard_map/ppermute | solution.py:10
  19.9 0.0 copy-done.6
  19.9 10.7 %collective-permute-done.1 = bf16[384,512]{1,0:T(8,128)(2,1)S(1)} collective-permute-done((bf16[384,512]{1,0:T(8,128)(2,1)S(1)}, bf16[384,512]{1,0:T(8,128)(2,1)S(1)}, u32[]{:S(2)}, u32[]{:S(2)}) %collective-permute-start.1) | collective-permute-done | bytes 393248 | tf_op jit(solution)/shard_map/ppermute | solution.py:10
  30.6 28.5 %all-gather.13.cloned.1.call-done = bf16[1,3,512,512]{2,3,1,0:T(8,128)(2,1)} async-done(((bf16[1,3,512,64]{2,3,1,0:T(8,128)(2,1)}), bf16[1,3,512,512]{2,3,1,0:T(8,128)(2,1)}) %all-gather.13.cloned.1.call-update) | async-done | bytes 1572880 | tf_op jit(solution)/shard_map/all_gather | solution.py:44
  59.0 1.4 fusion.62
  60.5 1.5 fusion.63
  62.0 0.0 collective-permute-done
  62.0 1.6 multiply_reduce_fusion.3
  63.6 47.5 %all-gather.15.cloned.1.call-done = bf16[1,512,2048]{2,1,0:T(8,128)(2,1)} async-done(((bf16[1,512,256]{2,1,0:T(8,128)(2,1)}), bf16[1,512,2048]{2,1,0:T(8,128)(2,1)}) %all-gather.15.cloned.1.call-update) | async-done | bytes 2097168 | tf_op jit(solution)/shard_map/all_gather | solution.py:50
  111.0 49.6 %all-gather.17.cloned.1.call-done = bf16[1,2048,512]{2,1,0:T(8,128)(2,1)} async-done(((bf16[1,256,512]{2,1,0:T(8,128)(2,1)}), bf16[1,2048,512]{2,1,0:T(8,128)(2,1)}) %all-gather.17.cloned.1.call-update) | async-done | bytes 2097168 | tf_op jit(solution)/shard_map/all_gather | solution.py:53
  160.7 4.4 %multiply_reduce_fusion.2 = (f32[384]{0:T(512)S(1)}, f32[384,512]{1,0:T(8,128)S(1)}) fusion(f32[384,512]{1,0:T(8,128)S(1)} %get-tuple-element.16, bf16[1,2048,512]{2,1,0:T(8,128)(2,1)} %all-gather.17.cloned.1.call-done, bf16[1,512,2048]{2,1,0:T(8,128)(2,1)} %all-gather.15.cloned.1.call-done, f32[512]{0:T(512)S(1)} %bitcast.91, f32[384]{0:T(512)S(1)} %add_rsqrt_fusion.3), kind=kOutput, calls=%fused_computation.62 | convolution fusion | flops 1618869888 | bytes 5772288 | tf_op jit(solution)/shard_map/dot_general | solution.py:22
  165.0 0.1 multiply_convert_fusion.4
  165.2 1.3 collective-permute-start.3
  166.5 5.5 %collective-permute-start.2 = (bf16[384,512]{1,0:T(8,128)(2,1)S(1)}, bf16[384,512]{1,0:T(8,128)(2,1)S(1)}, u32[]{:S(2)}, u32[]{:S(2)}) collective-permute-start(bf16[384,512]{1,0:T(8,128)(2,1)S(1)} %multiply_convert_fusion.4), channel_id=1, source_target_pairs={{0,8},{4,12},{1,9},{5,13},{2,10},{6,14},{3,11},{7,15},{16,24},{20,... | collective-permute-start | bytes 1179656 | tf_op jit(solution)/shard_map/ppermute | solution.py:10
  172.0 46.6 %all-gather.19.cloned.1.call-done = bf16[1,3,512,512]{2,3,1,0:T(8,128)(2,1)} async-done(((bf16[1,3,512,64]{2,3,1,0:T(8,128)(2,1)}), bf16[1,3,512,512]{2,3,1,0:T(8,128)(2,1)}) %all-gather.19.cloned.1.call-update) | async-done | bytes 1572880 | tf_op jit(solution)/shard_map/all_gather | solution.py:44
  218.6 1.4 fusion.61
  220.0 0.0 collective-permute-done.3
  220.1 1.4 fusion.60
  221.5 0.0 collective-permute-done.2
  221.5 1.6 multiply_reduce_fusion.1
  223.1 47.3 %all-gather.21.cloned.1.call-done = bf16[1,512,2048]{2,1,0:T(8,128)(2,1)} async-done(((bf16[1,512,256]{2,1,0:T(8,128)(2,1)}), bf16[1,512,2048]{2,1,0:T(8,128)(2,1)}) %all-gather.21.cloned.1.call-update) | async-done | bytes 2097168 | tf_op jit(solution)/shard_map/all_gather | solution.py:50
  270.4 49.5 %all-gather.23.cloned.1.call-done = bf16[1,2048,512]{2,1,0:T(8,128)(2,1)} async-done(((bf16[1,256,512]{2,1,0:T(8,128)(2,1)}), bf16[1,2048,512]{2,1,0:T(8,128)(2,1)}) %all-gather.23.cloned.1.call-update) | async-done | bytes 2097168 | tf_op jit(solution)/shard_map/all_gather | solution.py:53
  319.9 4.4 %multiply_reduce_fusion = (f32[384]{0:T(512)S(1)}, f32[384,512]{1,0:T(8,128)S(1)}) fusion(f32[384,512]{1,0:T(8,128)S(1)} %get-tuple-element.20, bf16[1,2048,512]{2,1,0:T(8,128)(2,1)} %all-gather.23.cloned.1.call-done, bf16[1,512,2048]{2,1,0:T(8,128)(2,1)} %all-gather.21.cloned.1.call-done, f32[512]{0:T(512)S(1)} %bitcast.90, f32[384]{0:T(512)S(1)} %add_rsqrt_fusion.1), kind=kOutput, calls=%fused_computation.58 | convolution fusion | flops 1618869888 | bytes 5772288 | tf_op jit(solution)/shard_map/dot_general | solution.py:22
  324.3 0.0 copy-done.7
  324.3 0.1 multiply_convert_fusion
  324.4 0.1 collective-permute-start.4
  324.5 1.7 collective-permute-done.4
  326.2 0.6 collective-permute-start.5
  326.8 10.6 %collective-permute-done.5 = bf16[384,512]{1,0:T(8,128)(2,1)S(1)} collective-permute-done((bf16[384,512]{1,0:T(8,128)(2,1)S(1)}, bf16[384,512]{1,0:T(8,128)(2,1)S(1)}, u32[]{:S(2)}, u32[]{:S(2)}) %collective-permute-start.5) | collective-permute-done | bytes 393248 | tf_op jit(solution)/shard_map/ppermute | solution.py:14
  337.4 1.5 collective-permute-start.6
  338.8 8.8 %collective-permute-done.6 = bf16[384,512]{1,0:T(8,128)(2,1)S(1)} collective-permute-done((bf16[384,512]{1,0:T(8,128)(2,1)S(1)}, bf16[384,512]{1,0:T(8,128)(2,1)S(1)}, u32[]{:S(2)}, u32[]{:S(2)}) %collective-permute-start.6) | collective-permute-done | bytes 393248 | tf_op jit(solution)/shard_map/ppermute | solution.py:14
  347.7 1.8 collective-permute-start.7
  349.5 16.9 %collective-permute-done.7 = bf16[384,512]{1,0:T(8,128)(2,1)S(1)} collective-permute-done((bf16[384,512]{1,0:T(8,128)(2,1)S(1)}, bf16[384,512]{1,0:T(8,128)(2,1)S(1)}, u32[]{:S(2)}, u32[]{:S(2)}) %collective-permute-start.7) | collective-permute-done | bytes 393248 | tf_op jit(solution)/shard_map/ppermute | solution.py:14
  366.4 0.5 rev.4
  366.9 0.0 copy-done
  366.9 0.0 copy-start.2
  366.9 0.0 copy-start.3
  366.9 0.5 fusion.47
  367.4 0.5 copy-done.2
  367.9 0.2 copy-done.3
  368.1 1.4 fusion.48
  (11 shorter events, 0.1 us)
Async XLA Ops:
  6.5 360.4 %copy-start = (bf16[512,512]{1,0:T(8,128)(2,1)S(1)}, bf16[512,512]{1,0:T(8,128)(2,1)}, u32[]{:S(2)}) copy-start(bf16[512,512]{1,0:T(8,128)(2,1)} %param.18) | copy-start | bytes 1572868
  6.5 4.0 %copy-start.4 = (bf16[2,256,512]{2,1,0:T(8,128)(2,1)S(1)}, bf16[2,256,512]{2,1,0:T(8,128)(2,1)}, u32[]{:S(2)}) copy-start(bf16[2,256,512]{2,1,0:T(8,128)(2,1)} %param.15) | copy-start | bytes 1572868
  6.5 6.1 %copy-start.1 = (bf16[1,384,512]{2,1,0:T(8,128)(2,1)S(1)}, bf16[1,384,512]{2,1,0:T(8,128)(2,1)}, u32[]{:S(2)}) copy-start(bf16[1,384,512]{2,1,0:T(8,128)(2,1)} %param.10) | copy-start | bytes 1179652
  6.5 6.2 %copy-start.5 = (f32[2,512]{1,0:T(2,128)S(1)}, f32[2,512]{1,0:T(2,128)}, u32[]{:S(2)}) copy-start(f32[2,512]{1,0:T(2,128)} %param.11) | copy-start | bytes 12292
  6.5 52.5 %all-gather.13.cloned.1.call-start = ((), (), s32[]{:S(2)}) async-start(), calls=%async_computation | async-start | bytes 1769472 | tf_op jit(solution)/shard_map/all_gather | solution.py:44
  8.5 11.3 %copy-start.6 = (f32[2,512]{1,0:T(2,128)S(1)}, f32[2,512]{1,0:T(2,128)}, u32[]{:S(2)}) copy-start(f32[2,512]{1,0:T(2,128)} %param.13) | copy-start | bytes 12292
  8.5 102.5 %all-gather.15.cloned.1.call-start = ((), (), s32[]{:S(2)}) async-start(), calls=%async_computation.1 | async-start | bytes 2359296 | tf_op jit(solution)/shard_map/all_gather | solution.py:50
  10.5 150.2 %all-gather.17.cloned.1.call-start = ((), (), s32[]{:S(2)}) async-start(), calls=%async_computation.2 | async-start | bytes 2359296 | tf_op jit(solution)/shard_map/all_gather | solution.py:53
  11.4 207.2 %all-gather.19.cloned.1.call-start = ((), (), s32[]{:S(2)}) async-start(), calls=%async_computation.3 | async-start | bytes 1769472 | tf_op jit(solution)/shard_map/all_gather | solution.py:44
  12.0 258.4 %all-gather.21.cloned.1.call-start = ((), (), s32[]{:S(2)}) async-start(), calls=%async_computation.4 | async-start | bytes 2359296 | tf_op jit(solution)/shard_map/all_gather | solution.py:50
  12.6 307.3 %all-gather.23.cloned.1.call-start = ((), (), s32[]{:S(2)}) async-start(), calls=%async_computation.5 | async-start | bytes 2359296 | tf_op jit(solution)/shard_map/all_gather | solution.py:53
  13.0 17.6 %collective-permute-start.1 = (bf16[384,512]{1,0:T(8,128)(2,1)S(1)}, bf16[384,512]{1,0:T(8,128)(2,1)S(1)}, u32[]{:S(2)}, u32[]{:S(2)}) collective-permute-start(bf16[384,512]{1,0:T(8,128)(2,1)S(1)} %fusion.57), channel_id=1, source_target_pairs={{4,0},{8,4},{12,8},{5,1},{9,5},{13,9},{6,2},{10,6},{14,10},{7,3},{... | collective-permute-start | bytes 1179656 | tf_op jit(solution)/shard_map/ppermute | solution.py:10
  14.3 47.7 %collective-permute-start = (bf16[384,512]{1,0:T(8,128)(2,1)S(1)}, bf16[384,512]{1,0:T(8,128)(2,1)S(1)}, u32[]{:S(2)}, u32[]{:S(2)}) collective-permute-start(bf16[384,512]{1,0:T(8,128)(2,1)S(1)} %fusion.57), channel_id=1, source_target_pairs={{0,4},{4,8},{8,12},{1,5},{5,9},{9,13},{2,6},{6,10},{10,14},{3,7},{... | collective-permute-start | bytes 1179656 | tf_op jit(solution)/shard_map/ppermute | solution.py:10
  165.2 54.9 %collective-permute-start.3 = (bf16[384,512]{1,0:T(8,128)(2,1)S(1)}, bf16[384,512]{1,0:T(8,128)(2,1)S(1)}, u32[]{:S(2)}, u32[]{:S(2)}) collective-permute-start(bf16[384,512]{1,0:T(8,128)(2,1)S(1)} %multiply_convert_fusion.4), channel_id=1, source_target_pairs={{8,0},{12,4},{9,1},{13,5},{10,2},{14,6},{11,3},{15,7},{24,16},{28,... | collective-permute-start | bytes 1179656 | tf_op jit(solution)/shard_map/ppermute | solution.py:10
  166.5 55.0 %collective-permute-start.2 = (bf16[384,512]{1,0:T(8,128)(2,1)S(1)}, bf16[384,512]{1,0:T(8,128)(2,1)S(1)}, u32[]{:S(2)}, u32[]{:S(2)}) collective-permute-start(bf16[384,512]{1,0:T(8,128)(2,1)S(1)} %multiply_convert_fusion.4), channel_id=1, source_target_pairs={{0,8},{4,12},{1,9},{5,13},{2,10},{6,14},{3,11},{7,15},{16,24},{20,... | collective-permute-start | bytes 1179656 | tf_op jit(solution)/shard_map/ppermute | solution.py:10
  319.9 4.4 %copy-start.7 = (f32[512]{0:T(512)S(1)}, f32[512]{0:T(512)}, u32[]{:S(2)}) copy-start(f32[512]{0:T(512)} %param.16) | copy-start | bytes 6148
  324.4 1.8 collective-permute-start.4
  326.2 11.2 %collective-permute-start.5 = (bf16[384,512]{1,0:T(8,128)(2,1)S(1)}, bf16[384,512]{1,0:T(8,128)(2,1)S(1)}, u32[]{:S(2)}, u32[]{:S(2)}) collective-permute-start(bf16[384,512]{1,0:T(8,128)(2,1)S(1)} %collective-permute-done.4), channel_id=1, source_target_pairs={{0,1},{1,0},{4,5},{5,4},{8,9},{9,8},{12,13},{13,12},{2,3},{3,2},{6... | collective-permute-start | bytes 1179656 | tf_op jit(solution)/shard_map/ppermute | solution.py:14
  337.4 10.3 %collective-permute-start.6 = (bf16[384,512]{1,0:T(8,128)(2,1)S(1)}, bf16[384,512]{1,0:T(8,128)(2,1)S(1)}, u32[]{:S(2)}, u32[]{:S(2)}) collective-permute-start(bf16[384,512]{1,0:T(8,128)(2,1)S(1)} %collective-permute-done.5), channel_id=1, source_target_pairs={{0,4},{1,5},{4,0},{5,1},{8,12},{9,13},{12,8},{13,9},{2,6},{3,7},{6... | collective-permute-start | bytes 1179656 | tf_op jit(solution)/shard_map/ppermute | solution.py:14
  347.7 18.7 %collective-permute-start.7 = (bf16[384,512]{1,0:T(8,128)(2,1)S(1)}, bf16[384,512]{1,0:T(8,128)(2,1)S(1)}, u32[]{:S(2)}, u32[]{:S(2)}) collective-permute-start(bf16[384,512]{1,0:T(8,128)(2,1)S(1)} %collective-permute-done.6), channel_id=1, source_target_pairs={{0,8},{1,9},{4,12},{5,13},{8,0},{9,1},{12,4},{13,5},{2,10},{3,11},... | collective-permute-start | bytes 1179656 | tf_op jit(solution)/shard_map/ppermute | solution.py:14
  366.9 1.0 copy-start.2
  366.9 1.2 copy-start.3
Sparse Core Ops, SparseCore 0:
  9.6 49.4 all-gather.12
  61.1 49.8 all-gather.14
  113.1 47.4 all-gather.16
  162.7 55.8 all-gather.18
  220.5 49.8 all-gather.20
  272.4 47.4 all-gather.22
where the time goes:
time: 377 us; the launch traced here: 376 us
  waiting for transfers between devices  319 us (85%)
  matrix products  19.5 us (5%)
  starting transfers between devices  17.8 us (5%)
  between operations  13.7 us (4%)
  local copies, waits for them, and re-layouts  5.8 us (2%)
    all_gather x2, waiting for transfers between devices, local(): lax.all_gather(down_weight[block], ('seq', 'chan'), axis=0, tiled=True)  99.1 us
    all_gather x2, waiting for transfers between devices, local(): lax.all_gather(up_weight[block], ('seq', 'chan'), axis=1, tiled=True)  94.8 us
    all_gather x2, waiting for transfers between devices, local(): lax.all_gather(conv_weight[block], ('seq', 'chan'), axis=2, tiled=True)  75.1 us
    ppermute x4, waiting for transfers between devices, swapped(): lax.ppermute(x, axis, [(i, i ^ 1 << stride) for i in range(lax.axis_size(...  38.1 us
    dot_general x10, matrix products, matmul(): return jnp.dot(left, right, preferred_element_type=jnp.float32)  19.5 us
    ppermute x4, starting transfers between devices, passed_along(): lax.ppermute(value, axis, [(source, source + steps) for source in range(i...  13.7 us
    ppermute x4, waiting for transfers between devices, passed_along(): lax.ppermute(value, axis, [(source, source + steps) for source in range(i...  10.7 us
  transfers between devices with their start and end apart: 14, of which 11 were waited for; matrix products, arithmetic and copies ran while one was open for 4% of the time, Pallas kernels for 0%

commit v1 on v0

--- a/solution.py
+++ b/solution.py
@@ -1,7 +1,25 @@
+import functools
 import jax
 import jax.numpy as jnp
 from jax import lax
 from jax.sharding import PartitionSpec as P
+
+
+def replace_results(x_in, dim_i):
+    big, tall = (lax.axis_size(("seq", "chan")), lax.axis_index(("seq", "chan")))
+    y1, upper = (x_in, 1)
+    while upper < big:
+        local_now = lax.ppermute(
+            y1, ("seq", "chan"), list(map(lambda h: (h, h ^ upper), range(big)))
+        )
+        now = jnp.concatenate([y1, local_now], axis=dim_i)
+        v_next = jnp.concatenate([local_now, y1], axis=dim_i)
+        y1 = jnp.where(tall & upper == 0, now, v_next)
+        upper = 2 * upper
+    return y1
+
+
+cover_the_set = functools.partial(replace_results, dim_i=1)
 
 
 def passed_along(value, axis, steps):
@@ -46,9 +64,7 @@
         conv = total.astype(jnp.bfloat16)
         state = state + conv.astype(jnp.float32)
         mixed = normalize(state, ff_norm[block]).astype(jnp.bfloat16)
-        hidden = jax.nn.gelu(
-            matmul(mixed, lax.all_gather(up_weight[block], ("seq", "chan"), axis=1, tiled=True))
-        ).astype(jnp.bfloat16)
+        hidden = jax.nn.gelu(matmul(mixed, cover_the_set(up_weight[block]))).astype(jnp.bfloat16)
         state = state + matmul(
             hidden, lax.all_gather(down_weight[block], ("seq", "chan"), axis=0, tiled=True)
         )

time: 377 us -> 336 us (0.89)
  waiting for transfers between devices: 319 us -> 262 us
  starting transfers between devices: 17.8 us -> 27.8 us
  other arithmetic: 0.63 us -> 4.69 us
    all_gather x2 -> x0, waiting for transfers between devices: 94.8 us -> none  [local(): lax.all_gather(up_weight[block], ('seq', 'chan'), axis=1, tiled=True)]
    ppermute x0 -> x6, waiting for transfers between devices: none -> 45.1 us  [replace_results(): lax.ppermute(y1, ('seq', 'chan'), list(map(lambda h: (h, h ^ upper), rang...]
    ppermute x4, waiting for transfers between devices: 10.7 us -> 34.1 us  [passed_along(): lax.ppermute(value, axis, [(source, source + steps) for source in range(i...]
    all_gather x2, waiting for transfers between devices: 99.1 us -> 79.4 us  [local(): lax.all_gather(down_weight[block], ('seq', 'chan'), axis=0, tiled=True)]
    ppermute x0 -> x6, starting transfers between devices: none -> 13.2 us  [replace_results(): lax.ppermute(y1, ('seq', 'chan'), list(map(lambda h: (h, h ^ upper), rang...]
    all_gather x2, waiting for transfers between devices: 75.1 us -> 65.1 us  [local(): lax.all_gather(conv_weight[block], ('seq', 'chan'), axis=2, tiled=True)]
  transfers between devices with their start and end apart: 14 -> 18, of which waited for: 11 -> 13; matrix products, arithmetic and copies ran while one was open for 4% -> 7% of each run, Pallas kernels for 0% -> 0%
where the time goes in v1:
time: 336 us; the launch traced here: 335 us
  waiting for transfers between devices  262 us (78%)
  starting transfers between devices  27.8 us (8%)
  matrix products  21.4 us (6%)
  between operations  13.4 us (4%)
  local copies, waits for them, and re-layouts  5.58 us (2%)
  other arithmetic  4.69 us (1%)
    all_gather x2, waiting for transfers between devices, local(): lax.all_gather(down_weight[block], ('seq', 'chan'), axis=0, tiled=True)  79.4 us
    all_gather x2, waiting for transfers between devices, local(): lax.all_gather(conv_weight[block], ('seq', 'chan'), axis=2, tiled=True)  65.1 us
    ppermute x6, waiting for transfers between devices, replace_results(): lax.ppermute(y1, ('seq', 'chan'), list(map(lambda h: (h, h ^ upper), rang...  45.1 us
    ppermute x4, waiting for transfers between devices, swapped(): lax.ppermute(x, axis, [(i, i ^ 1 << stride) for i in range(lax.axis_size(...  38.1 us
    ppermute x4, waiting for transfers between devices, passed_along(): lax.ppermute(value, axis, [(source, source + steps) for source in range(i...  34.1 us
    dot_general x10, matrix products, matmul(): return jnp.dot(left, right, preferred_element_type=jnp.float32)  21.4 us
    ppermute x6, starting transfers between devices, replace_results(): lax.ppermute(y1, ('seq', 'chan'), list(map(lambda h: (h, h ^ upper), rang...  13.2 us
    ppermute x4, starting transfers between devices, passed_along(): lax.ppermute(value, axis, [(source, source + steps) for source in range(i...  10.5 us
  transfers between devices with their start and end apart: 18, of which 13 were waited for; matrix products, arithmetic and copies ran while one was open for 7% of the time, Pallas kernels for 0%

profile of v1, /device:TPU:0, one launch (start us, length us, event | category | flops | bytes accessed | tf_op | source)
XLA Modules:
  0.0 335.3 jit_solution(11896056782516662570)
XLA Ops:
  6.5 0.0 all-gather.9.cloned.1.call-start
  6.6 1.9 fusion.91
  8.5 0.0 all-gather.9.cloned.1.call-update
  8.6 0.0 all-gather.11.cloned.1.call-start
  8.6 1.9 fusion.90
  10.5 0.0 all-gather.11.cloned.1.call-update
  10.5 0.0 all-gather.13.cloned.1.call-start
  10.6 0.7 all-gather.13.cloned.1.call-update
  11.3 0.0 all-gather.15.cloned.1.call-start
  11.4 3.0 collective-permute-start.2
  14.4 0.1 collective-permute-start.7
  14.4 0.2 fusion.57
  14.6 6.9 %collective-permute-done.2 = bf16[512,256]{1,0:T(8,128)(2,1)S(1)} collective-permute-done((bf16[512,256]{1,0:T(8,128)(2,1)S(1)}, bf16[512,256]{1,0:T(8,128)(2,1)S(1)}, u32[]{:S(2)}, u32[]{:S(2)}) %collective-permute-start.2) | collective-permute-done | bytes 262176 | tf_op jit(solution)/shard_map/ppermute | solution.py:12
  21.5 0.1 maximum_select_fusion.14
  21.6 2.2 collective-permute-start.3
  23.8 0.9 fusion.59
  24.7 1.3 collective-permute-start.1
  26.0 5.3 %collective-permute-start = (bf16[384,512]{1,0:T(8,128)(2,1)}, bf16[384,512]{1,0:T(8,128)(2,1)}, u32[]{:S(2)}, u32[]{:S(2)}) collective-permute-start(bf16[384,512]{1,0:T(8,128)(2,1)} %fusion.59), channel_id=1, source_target_pairs={{0,4},{4,8},{8,12},{1,5},{5,9},{9,13},{2,6},{6,10},{10,14},{3,7},{... | collective-permute-start | bytes 1179656 | tf_op jit(solution)/shard_map/ppermute | solution.py:28
  31.3 0.0 all-gather.15.cloned.1.call-update
  31.4 0.5 fusion.92
  31.9 0.1 maximum_select_fusion.15
  32.0 0.5 collective-permute-start.8
  32.5 8.6 %collective-permute-done.3 = bf16[512,512]{1,0:T(8,128)(2,1)} collective-permute-done((bf16[512,512]{1,0:T(8,128)(2,1)S(1)}, bf16[512,512]{1,0:T(8,128)(2,1)}, u32[]{:S(2)}, u32[]{:S(2)}) %collective-permute-start.3) | collective-permute-done | bytes 524320 | tf_op jit(solution)/shard_map/ppermute | solution.py:12
  41.1 1.5 maximum_select_fusion.8
  42.6 3.1 collective-permute-start.4
  45.7 34.1 %collective-permute-done.1 = bf16[384,512]{1,0:T(8,128)(2,1)} collective-permute-done((bf16[384,512]{1,0:T(8,128)(2,1)}, bf16[384,512]{1,0:T(8,128)(2,1)}, u32[]{:S(2)}, u32[]{:S(2)}) %collective-permute-start.1) | collective-permute-done | bytes 393248 | tf_op jit(solution)/shard_map/ppermute | solution.py:28
  79.8 0.2 all-gather.9.cloned.1.call-done
  80.0 1.6 fusion.64
  81.6 1.5 fusion.65
  83.1 2.6 multiply_reduce_fusion.3
  85.7 24.1 %collective-permute-done.4 = bf16[512,1024]{1,0:T(8,128)(2,1)} collective-permute-done((bf16[512,1024]{1,0:T(8,128)(2,1)S(1)}, bf16[512,1024]{1,0:T(8,128)(2,1)}, u32[]{:S(2)}, u32[]{:S(2)}) %collective-permute-start.4) | collective-permute-done | bytes 1048608 | tf_op jit(solution)/shard_map/ppermute | solution.py:12
  109.7 27.2 %all-gather.11.cloned.1.call-done = bf16[1,2048,512]{2,1,0:T(8,128)(2,1)} async-done(((bf16[1,256,512]{2,1,0:T(8,128)(2,1)}), bf16[1,2048,512]{2,1,0:T(8,128)(2,1)}) %all-gather.11.cloned.1.call-update) | async-done | bytes 2097168 | tf_op jit(solution)/shard_map/all_gather | solution.py:69
  137.0 4.9 %multiply_reduce_fusion.2 = (f32[384]{0:T(512)S(1)}, f32[384,512]{1,0:T(8,128)S(1)}) fusion(f32[384,512]{1,0:T(8,128)} %get-tuple-element.16, bf16[1,2048,512]{2,1,0:T(8,128)(2,1)} %all-gather.11.cloned.1.call-done, bf16[512,1024]{1,0:T(8,128)(2,1)} %collective-permute-done.4, bf16[512,1024]{1,0:T(8,128)(2,1)S(1)} %maximum_select_fusion.8, pred[]{:T(512)S(6)} %eq.12, ...), kind=kOutput, calls=%fused_computation.76 | convolution fusion | flops 1628307072 | bytes 5772289 | tf_op jit(solution)/shard_map/dot_general | solution.py:40
  141.9 0.1 multiply_convert_fusion.4
  142.0 1.3 collective-permute-start.6
  143.3 0.0 collective-permute-done.8
  143.3 1.5 maximum_select_fusion.9
  144.9 4.4 %collective-permute-start.9 = (bf16[512,1024]{1,0:T(8,128)(2,1)S(1)}, bf16[512,1024]{1,0:T(8,128)(2,1)}, u32[]{:S(2)}, u32[]{:S(2)}) collective-permute-start(bf16[512,1024]{1,0:T(8,128)(2,1)S(1)} %maximum_select_fusion.9), channel_id=1, source_target_pairs={{0,8},{1,9},{4,12},{5,13},{8,0},{9,1},{12,4},{13,5},{2,10},{3,11},... | collective-permute-start | bytes 3145736 | tf_op jit(solution)/shard_map/ppermute | solution.py:12
  149.2 2.7 collective-permute-start.5
  151.9 64.8 %all-gather.13.cloned.1.call-done = bf16[1,3,512,512]{2,3,1,0:T(8,128)(2,1)} async-done(((bf16[1,3,512,64]{2,3,1,0:T(8,128)(2,1)}), bf16[1,3,512,512]{2,3,1,0:T(8,128)(2,1)}) %all-gather.13.cloned.1.call-update) | async-done | bytes 1572880 | tf_op jit(solution)/shard_map/all_gather | solution.py:62
  216.8 1.4 fusion.63
  218.2 0.0 collective-permute-done.6
  218.2 1.6 fusion.62
  219.8 0.0 collective-permute-done.5
  219.8 1.7 multiply_reduce_fusion.1
  221.5 5.6 %collective-permute-done.9 = bf16[512,1024]{1,0:T(8,128)(2,1)} collective-permute-done((bf16[512,1024]{1,0:T(8,128)(2,1)S(1)}, bf16[512,1024]{1,0:T(8,128)(2,1)}, u32[]{:S(2)}, u32[]{:S(2)}) %collective-permute-start.9) | collective-permute-done | bytes 1048608 | tf_op jit(solution)/shard_map/ppermute | solution.py:12
  227.0 52.2 %all-gather.15.cloned.1.call-done = bf16[1,2048,512]{2,1,0:T(8,128)(2,1)} async-done(((bf16[1,256,512]{2,1,0:T(8,128)(2,1)}), bf16[1,2048,512]{2,1,0:T(8,128)(2,1)}) %all-gather.15.cloned.1.call-update) | async-done | bytes 2097168 | tf_op jit(solution)/shard_map/all_gather | solution.py:69
  279.2 4.4 %multiply_reduce_fusion = (f32[384]{0:T(512)S(1)}, f32[384,512]{1,0:T(8,128)S(1)}) fusion(f32[384,512]{1,0:T(8,128)S(1)} %get-tuple-element.20, bf16[1,2048,512]{2,1,0:T(8,128)(2,1)} %all-gather.15.cloned.1.call-done, bf16[512,1024]{1,0:T(8,128)(2,1)} %collective-permute-done.9, bf16[512,1024]{1,0:T(8,128)(2,1)S(1)} %maximum_select_fusion.9, pred[]{:T(512)S(6)} %eq.12, ...), kind=kOutput, calls=%fused_computation.72 | convolution fusion | flops 1628307072 | bytes 5772289 | tf_op jit(solution)/shard_map/dot_general | solution.py:40
  283.6 0.1 multiply_convert_fusion
  283.8 0.1 collective-permute-start.10
  283.8 1.7 collective-permute-done.10
  285.5 0.6 collective-permute-start.11
  286.1 10.6 %collective-permute-done.11 = bf16[384,512]{1,0:T(8,128)(2,1)S(1)} collective-permute-done((bf16[384,512]{1,0:T(8,128)(2,1)S(1)}, bf16[384,512]{1,0:T(8,128)(2,1)S(1)}, u32[]{:S(2)}, u32[]{:S(2)}) %collective-permute-start.11) | collective-permute-done | bytes 393248 | tf_op jit(solution)/shard_map/ppermute | solution.py:32
  296.7 1.5 collective-permute-start.12
  298.2 8.8 %collective-permute-done.12 = bf16[384,512]{1,0:T(8,128)(2,1)S(1)} collective-permute-done((bf16[384,512]{1,0:T(8,128)(2,1)S(1)}, bf16[384,512]{1,0:T(8,128)(2,1)S(1)}, u32[]{:S(2)}, u32[]{:S(2)}) %collective-permute-start.12) | collective-permute-done | bytes 393248 | tf_op jit(solution)/shard_map/ppermute | solution.py:32
  307.0 1.8 collective-permute-start.13
  308.8 16.9 %collective-permute-done.13 = bf16[384,512]{1,0:T(8,128)(2,1)S(1)} collective-permute-done((bf16[384,512]{1,0:T(8,128)(2,1)S(1)}, bf16[384,512]{1,0:T(8,128)(2,1)S(1)}, u32[]{:S(2)}, u32[]{:S(2)}) %collective-permute-start.13) | collective-permute-done | bytes 393248 | tf_op jit(solution)/shard_map/ppermute | solution.py:32
  325.8 0.5 rev.4
  326.2 0.0 copy-start.2
  326.2 0.0 copy-start.3
  326.3 0.5 fusion.53
  326.7 0.5 copy-done.2
  327.3 0.2 copy-done.3
  327.4 1.4 fusion.54
  (23 shorter events, 0.1 us)
Async XLA Ops:
  6.5 319.7 %copy-start = (bf16[512,512]{1,0:T(8,128)(2,1)S(1)}, bf16[512,512]{1,0:T(8,128)(2,1)}, u32[]{:S(2)}) copy-start(bf16[512,512]{1,0:T(8,128)(2,1)} %param.18) | copy-start | bytes 1572868
  6.5 4.8 %copy-start.4 = (bf16[2,512,256]{2,1,0:T(8,128)(2,1)S(1)}, bf16[2,512,256]{2,1,0:T(8,128)(2,1)}, u32[]{:S(2)}) copy-start(bf16[2,512,256]{2,1,0:T(8,128)(2,1)} %param.14) | copy-start | bytes 1572868
  6.5 7.9 %copy-start.1 = (bf16[1,384,512]{2,1,0:T(8,128)(2,1)S(1)}, bf16[1,384,512]{2,1,0:T(8,128)(2,1)}, u32[]{:S(2)}) copy-start(bf16[1,384,512]{2,1,0:T(8,128)(2,1)} %param.10) | copy-start | bytes 1179652
  6.5 8.1 %copy-start.5 = (f32[2,512]{1,0:T(2,128)S(1)}, f32[2,512]{1,0:T(2,128)}, u32[]{:S(2)}) copy-start(f32[2,512]{1,0:T(2,128)} %param.11) | copy-start | bytes 12292
  6.5 73.5 %all-gather.9.cloned.1.call-start = ((), (), s32[]{:S(2)}) async-start(), calls=%async_computation | async-start | bytes 1769472 | tf_op jit(solution)/shard_map/all_gather | solution.py:62
  8.6 128.4 %all-gather.11.cloned.1.call-start = ((), (), s32[]{:S(2)}) async-start(), calls=%async_computation.1 | async-start | bytes 2359296 | tf_op jit(solution)/shard_map/all_gather | solution.py:69
  10.5 20.9 %copy-start.6 = (f32[2,512]{1,0:T(2,128)S(1)}, f32[2,512]{1,0:T(2,128)}, u32[]{:S(2)}) copy-start(f32[2,512]{1,0:T(2,128)} %param.13) | copy-start | bytes 12292
  10.5 206.2 %all-gather.13.cloned.1.call-start = ((), (), s32[]{:S(2)}) async-start(), calls=%async_computation.2 | async-start | bytes 1769472 | tf_op jit(solution)/shard_map/all_gather | solution.py:62
  11.3 267.9 %all-gather.15.cloned.1.call-start = ((), (), s32[]{:S(2)}) async-start(), calls=%async_computation.3 | async-start | bytes 2359296 | tf_op jit(solution)/shard_map/all_gather | solution.py:69
  11.4 10.1 %collective-permute-start.2 = (bf16[512,256]{1,0:T(8,128)(2,1)S(1)}, bf16[512,256]{1,0:T(8,128)(2,1)S(1)}, u32[]{:S(2)}, u32[]{:S(2)}) collective-permute-start(bf16[512,256]{1,0:T(8,128)(2,1)S(1)} %get-tuple-element.6), channel_id=1, source_target_pairs={{0,1},{1,0},{4,5},{5,4},{8,9},{9,8},{12,13},{13,12},{2,3},{3,2},{6... | collective-permute-start | bytes 786440 | tf_op jit(solution)/shard_map/ppermute | solution.py:12
  14.4 17.5 %collective-permute-start.7 = (bf16[512,256]{1,0:T(8,128)(2,1)S(1)}, bf16[512,256]{1,0:T(8,128)(2,1)S(1)}, u32[]{:S(2)}, u32[]{:S(2)}) collective-permute-start(bf16[512,256]{1,0:T(8,128)(2,1)S(1)} %get-tuple-element.5), channel_id=1, source_target_pairs={{0,1},{1,0},{4,5},{5,4},{8,9},{9,8},{12,13},{13,12},{2,3},{3,2},{6... | collective-permute-start | bytes 786440 | tf_op jit(solution)/shard_map/ppermute | solution.py:12
  21.6 19.5 %collective-permute-start.3 = (bf16[512,512]{1,0:T(8,128)(2,1)S(1)}, bf16[512,512]{1,0:T(8,128)(2,1)}, u32[]{:S(2)}, u32[]{:S(2)}) collective-permute-start(bf16[512,512]{1,0:T(8,128)(2,1)S(1)} %maximum_select_fusion.14), channel_id=1, source_target_pairs={{0,4},{1,5},{4,0},{5,1},{8,12},{9,13},{12,8},{13,9},{2,6},{3,7},{6... | collective-permute-start | bytes 1572872 | tf_op jit(solution)/shard_map/ppermute | solution.py:12
  24.7 55.0 %collective-permute-start.1 = (bf16[384,512]{1,0:T(8,128)(2,1)}, bf16[384,512]{1,0:T(8,128)(2,1)}, u32[]{:S(2)}, u32[]{:S(2)}) collective-permute-start(bf16[384,512]{1,0:T(8,128)(2,1)} %fusion.59), channel_id=1, source_target_pairs={{4,0},{8,4},{12,8},{5,1},{9,5},{13,9},{6,2},{10,6},{14,10},{7,3},{... | collective-permute-start | bytes 1179656 | tf_op jit(solution)/shard_map/ppermute | solution.py:28
  26.0 57.0 %collective-permute-start = (bf16[384,512]{1,0:T(8,128)(2,1)}, bf16[384,512]{1,0:T(8,128)(2,1)}, u32[]{:S(2)}, u32[]{:S(2)}) collective-permute-start(bf16[384,512]{1,0:T(8,128)(2,1)} %fusion.59), channel_id=1, source_target_pairs={{0,4},{4,8},{8,12},{1,5},{5,9},{9,13},{2,6},{6,10},{10,14},{3,7},{... | collective-permute-start | bytes 1179656 | tf_op jit(solution)/shard_map/ppermute | solution.py:28
  32.0 111.3 %collective-permute-start.8 = (bf16[512,512]{1,0:T(8,128)(2,1)S(1)}, bf16[512,512]{1,0:T(8,128)(2,1)}, u32[]{:S(2)}, u32[]{:S(2)}) collective-permute-start(bf16[512,512]{1,0:T(8,128)(2,1)S(1)} %maximum_select_fusion.15), channel_id=1, source_target_pairs={{0,4},{1,5},{4,0},{5,1},{8,12},{9,13},{12,8},{13,9},{2,6},{3,7},{6... | collective-permute-start | bytes 1572872 | tf_op jit(solution)/shard_map/ppermute | solution.py:12
  42.6 67.1 %collective-permute-start.4 = (bf16[512,1024]{1,0:T(8,128)(2,1)S(1)}, bf16[512,1024]{1,0:T(8,128)(2,1)}, u32[]{:S(2)}, u32[]{:S(2)}) collective-permute-start(bf16[512,1024]{1,0:T(8,128)(2,1)S(1)} %maximum_select_fusion.8), channel_id=1, source_target_pairs={{0,8},{1,9},{4,12},{5,13},{8,0},{9,1},{12,4},{13,5},{2,10},{3,11},... | collective-permute-start | bytes 3145736 | tf_op jit(solution)/shard_map/ppermute | solution.py:12
  83.0 53.9 %copy-start.8 = (f32[1,512]{1,0:T(1,128)S(1)}, f32[1,512]{1,0:T(1,128)}, u32[]{:S(2)}) copy-start(f32[1,512]{1,0:T(1,128)} %get-tuple-element.12) | copy-start | bytes 6148
  142.0 76.2 %collective-permute-start.6 = (bf16[384,512]{1,0:T(8,128)(2,1)S(1)}, bf16[384,512]{1,0:T(8,128)(2,1)}, u32[]{:S(2)}, u32[]{:S(2)}) collective-permute-start(bf16[384,512]{1,0:T(8,128)(2,1)S(1)} %multiply_convert_fusion.4), channel_id=1, source_target_pairs={{8,0},{12,4},{9,1},{13,5},{10,2},{14,6},{11,3},{15,7},{24,16},{28,... | collective-permute-start | bytes 1179656 | tf_op jit(solution)/shard_map/ppermute | solution.py:28
  144.9 82.2 %collective-permute-start.9 = (bf16[512,1024]{1,0:T(8,128)(2,1)S(1)}, bf16[512,1024]{1,0:T(8,128)(2,1)}, u32[]{:S(2)}, u32[]{:S(2)}) collective-permute-start(bf16[512,1024]{1,0:T(8,128)(2,1)S(1)} %maximum_select_fusion.9), channel_id=1, source_target_pairs={{0,8},{1,9},{4,12},{5,13},{8,0},{9,1},{12,4},{13,5},{2,10},{3,11},... | collective-permute-start | bytes 3145736 | tf_op jit(solution)/shard_map/ppermute | solution.py:12
  149.2 70.5 %collective-permute-start.5 = (bf16[384,512]{1,0:T(8,128)(2,1)S(1)}, bf16[384,512]{1,0:T(8,128)(2,1)}, u32[]{:S(2)}, u32[]{:S(2)}) collective-permute-start(bf16[384,512]{1,0:T(8,128)(2,1)S(1)} %multiply_convert_fusion.4), channel_id=1, source_target_pairs={{0,8},{4,12},{1,9},{5,13},{2,10},{6,14},{3,11},{7,15},{16,24},{20,... | collective-permute-start | bytes 1179656 | tf_op jit(solution)/shard_map/ppermute | solution.py:28
  279.2 4.4 %copy-start.7 = (f32[512]{0:T(512)S(1)}, f32[512]{0:T(512)}, u32[]{:S(2)}) copy-start(f32[512]{0:T(512)} %param.16) | copy-start | bytes 6148
  283.8 1.8 collective-permute-start.10
  285.5 11.2 %collective-permute-start.11 = (bf16[384,512]{1,0:T(8,128)(2,1)S(1)}, bf16[384,512]{1,0:T(8,128)(2,1)S(1)}, u32[]{:S(2)}, u32[]{:S(2)}) collective-permute-start(bf16[384,512]{1,0:T(8,128)(2,1)S(1)} %collective-permute-done.10), channel_id=1, source_target_pairs={{0,1},{1,0},{4,5},{5,4},{8,9},{9,8},{12,13},{13,12},{2,3},{3,2},{6... | collective-permute-start | bytes 1179656 | tf_op jit(solution)/shard_map/ppermute | solution.py:32
  296.7 10.3 %collective-permute-start.12 = (bf16[384,512]{1,0:T(8,128)(2,1)S(1)}, bf16[384,512]{1,0:T(8,128)(2,1)S(1)}, u32[]{:S(2)}, u32[]{:S(2)}) collective-permute-start(bf16[384,512]{1,0:T(8,128)(2,1)S(1)} %collective-permute-done.11), channel_id=1, source_target_pairs={{0,4},{1,5},{4,0},{5,1},{8,12},{9,13},{12,8},{13,9},{2,6},{3,7},{6... | collective-permute-start | bytes 1179656 | tf_op jit(solution)/shard_map/ppermute | solution.py:32
  307.0 18.7 %collective-permute-start.13 = (bf16[384,512]{1,0:T(8,128)(2,1)S(1)}, bf16[384,512]{1,0:T(8,128)(2,1)S(1)}, u32[]{:S(2)}, u32[]{:S(2)}) collective-permute-start(bf16[384,512]{1,0:T(8,128)(2,1)S(1)} %collective-permute-done.12), channel_id=1, source_target_pairs={{0,8},{1,9},{4,12},{5,13},{8,0},{9,1},{12,4},{13,5},{2,10},{3,11},... | collective-permute-start | bytes 1179656 | tf_op jit(solution)/shard_map/ppermute | solution.py:32
  326.2 1.0 copy-start.2
  326.2 1.2 copy-start.3
Sparse Core Ops, SparseCore 0:
  9.6 70.4 all-gather.8
  82.1 54.7 all-gather.10
  139.2 77.5 all-gather.12
  218.7 60.4 all-gather.14
